TPU v7x, 256 devices: a whole 4x4x8 slice. The times are simulated.
256 devices in a mesh: front: 16 (over z, core), tile: 16 (over y, x).
Axes of the slice: x: 4, y: 4, z: 8, core: 2. Of those that a mesh axis runs over, the one named last changes fastest.
Arguments:
- pieces: bfloat16 [18432, 256, 128], P(('front', 'tile')), may hold values from -1.59375 to 1.59375
- dest_front: int32 [18432, 1], P(('front', 'tile')), may hold values from 0 to 15; in each aligned block of 72 rows (0 to 71, 72 to 143, ...) at most 9 rows name the same one
- dest_slot: int32 [18432], P(('front', 'tile')), may hold values from 0 to 3
- parent_u: bfloat16 [4096, 4096], P('front', 'tile'), may hold values from -1.59375 to 1.59375
- parent_v: bfloat16 [4096, 4096], P('front', 'tile'), may hold values from -1.59375 to 1.59375
- sketch: bfloat16 [256, 64], replicated, may hold values from -6 to 6
- pivot_inverse: bfloat16 [4096, 256], P('front'), may hold values from -0.01171875 to 0.01171875
Outputs:
- coeff: bfloat16 [4096, 4096], P('front', 'tile')
- cores: float32 [65536, 4096], P(('front', 'tile'))
Inputs may be any that keep to these rules, and one draw needn't show every extreme that they name: `dest_front`: among the 72 rows of one device at most 9 name any one front, a bound that some block reaches.
All inputs are finite; a program needn't handle non-finite values.
Results may differ from a plain program's by a relative error of at most 0.017.
Values may be sent and summed in bfloat16 or wider, within the bound.
No kernel may reach another device: no remote copies, remote signals or barrier semaphores. Data moves between devices by JAX's collectives and lax.ppermute only.
A program may use at most 128 MiB of HBM per device.

v0:
```python
import jax
import jax.numpy as jnp
from jax import lax
from jax.sharding import PartitionSpec as P

B = 256
R = 64
TILES_DEV = 4
CAP = 9


def sketch_pass(arrived, sketch):
    left_rows = arrived[..., :R]
    right_rows = arrived[..., R:]
    small = jnp.einsum(
        "...br,bk->...rk", right_rows, sketch, preferred_element_type=jnp.float32
    ).astype(jnp.bfloat16)
    return jnp.einsum("...br,...rk->...bk", left_rows, small, preferred_element_type=jnp.float32)


def orthonormal_basis(block_unit):
    gram_matrix = jnp.einsum(
        "naj,nav->njv", block_unit, block_unit, precision=lax.Precision.HIGHEST
    )
    lower = jnp.linalg.cholesky(gram_matrix)
    solved = jax.scipy.linalg.solve_triangular(lower, jnp.swapaxes(block_unit, 1, 2), lower=True)
    return jnp.swapaxes(solved, 1, 2)


def expand(factor, small):
    return jnp.einsum("pbr,prk->pbk", factor, small, preferred_element_type=jnp.float32)


def project(factor, other):
    return jnp.einsum("pbr,pbk->prk", factor, other, preferred_element_type=jnp.float32).astype(
        jnp.bfloat16
    )


def shards(pieces, dest_front, dest_slot, parent_u, parent_v, sketch, pivot_inverse):
    fronts = lax.axis_size("front")
    front_ids = dest_front[:, 0]
    front_marks = (front_ids[:, None] == jnp.arange(fronts, dtype=jnp.int32)[None, :]).astype(
        jnp.int32
    )
    prior_level = jnp.sum((jnp.cumsum(front_marks, axis=0) - front_marks) * front_marks, axis=1)
    places = front_ids * CAP + prior_level
    outgoing = (
        jnp.zeros((fronts * CAP, B, 2 * R), jnp.bfloat16)
        .at[places]
        .set(pieces)
        .reshape(fronts, CAP, B, 2 * R)
    )
    out_slots = (
        jnp.full((fronts * CAP,), TILES_DEV, jnp.int32)
        .at[places]
        .set(dest_slot)
        .reshape(fronts, CAP)
    )
    received, slot_ids = (
        lax.all_to_all(outgoing, "front", split_axis=0, concat_axis=0, tiled=True),
        lax.all_to_all(out_slots, "front", split_axis=0, concat_axis=0, tiled=True),
    )
    sketched = sketch_pass(received, sketch)
    slot_count = fronts * CAP
    piece_left = received[..., :R].reshape(slot_count, B, R)
    piece_right = received[..., R:].reshape(slot_count, B, R)
    sketched = sketched.reshape(slot_count, B, R)
    owner_mask = (
        slot_ids.reshape(slot_count)[None, :] == jnp.arange(TILES_DEV, dtype=jnp.int32)[:, None]
    )
    owner_float = owner_mask.astype(jnp.float32)
    owner_halves = owner_mask.astype(jnp.bfloat16)
    owned_left_rows = parent_u.reshape(B, TILES_DEV, R).transpose(1, 0, 2)
    own_right = parent_v.reshape(B, TILES_DEV, R).transpose(1, 0, 2)

    def collect(per_piece, parent_term):
        return (
            jnp.einsum("sp,pbk->sbk", owner_float, per_piece, precision=lax.Precision.HIGHEST)
            + parent_term
        )

    def select(field_values):
        return jnp.einsum(
            "eo,elj->olj", owner_halves, field_values, preferred_element_type=jnp.float32
        ).astype(jnp.bfloat16)

    y_start = collect(
        sketched, sketch_pass(jnp.concatenate((owned_left_rows, own_right), axis=2), sketch)
    )
    q_start = orthonormal_basis(y_start).astype(jnp.bfloat16)
    z_mid = collect(
        expand(piece_right, project(piece_left, select(q_start))),
        expand(own_right, project(owned_left_rows, q_start)),
    ).astype(jnp.bfloat16)
    y_end = collect(
        expand(piece_left, project(piece_right, select(z_mid))),
        expand(owned_left_rows, project(own_right, z_mid)),
    )
    q_end = orthonormal_basis(y_end).astype(jnp.bfloat16)
    w_end = collect(
        expand(piece_right, project(piece_left, select(q_end))),
        expand(own_right, project(owned_left_rows, q_end)),
    ).astype(jnp.bfloat16)
    coeff = w_end.transpose(1, 0, 2).reshape(B, TILES_DEV * R)
    pivoted = jnp.dot(pivot_inverse, coeff, preferred_element_type=jnp.float32).astype(jnp.bfloat16)
    cores = jnp.einsum(
        "bi,bj->ij",
        coeff,
        lax.all_gather(pivoted, "tile", axis=1, tiled=True),
        preferred_element_type=jnp.float32,
    )
    return (coeff, cores)


def solution(mesh):
    return jax.shard_map(
        shards,
        mesh=mesh,
        in_specs=(
            P(("front", "tile"), None, None),
            P(("front", "tile"), None),
            P(("front", "tile")),
            P("front", "tile"),
            P("front", "tile"),
            P(),
            P("front", None),
        ),
        out_specs=(P("front", "tile"), P(("front", "tile"), None)),
        check_vma=False,
    )
```

profile of v0, /device:TPU:2, one launch (start us, length us, event | category | flops | bytes accessed | tf_op | source)
XLA Modules:
  0.0 533.4 jit_solution(12885000864077269159)
XLA Ops:
  11.2 8.6 %all-to-all-start = ((s32[16,1,9]{2,1,0:T(1,128)}), s32[16,1,9]{2,1,0:T(1,128)S(1)}, u32[]{:S(2)}, u32[]{:S(2)}) async-start(s32[16,1,9]{2,1,0:T(1,128)} %bitcast.3), calls=%async_computation | async-start | bytes 16384 | tf_op jit(solution)/shard_map/all_to_all | solution.py:62
  19.8 6.0 %broadcast_in_dim.7 = bf16[144,256,128]{2,1,0:T(8,128)(2,1)} broadcast(bf16[]{:T(256)} %constant.46.clone.1), dimensions={} | broadcast | bytes 9437186 | tf_op jit(solution)/shard_map/broadcast_in_dim | solution.py:49
  25.8 14.6 %scatter_fusion = bf16[144,256,128]{2,1,0:T(8,128)(2,1)} fusion(bf16[144,256,128]{2,1,0:T(8,128)(2,1)} %broadcast_in_dim.7, s32[72]{0:T(128)S(1)} %fusion.76, bf16[72,256,128]{2,1,0:T(8,128)(2,1)} %param.10), kind=kCustom, calls=%fused_computation.1 | custom fusion | bytes 14156064 | tf_op jit(solution)/shard_map/scatter | solution.py:51
  40.3 12.7 %copy.125 = bf16[144,256,128]{1,2,0:T(8,128)(2,1)} copy(bf16[144,256,128]{2,1,0:T(8,128)(2,1)} %scatter_fusion) | data formatting | bytes 18874368 | tf_op jit(solution)/shard_map/scatter | solution.py:51
  53.1 7.4 %all-to-all-start.1 = ((bf16[16,9,256,128]{2,3,1,0:T(8,128)(2,1)}), bf16[16,9,256,128]{2,3,1,0:T(8,128)(2,1)}, u32[]{:S(2)}, u32[]{:S(2)}) async-start(bf16[16,9,256,128]{2,3,1,0:T(8,128)(2,1)} %bitcast.111), calls=%async_computation.1 | async-start | bytes 18874368 | tf_op jit(solution)/shard_map/all_to_all | solution.py:61
  62.6 204.5 %all-to-all-done.1 = bf16[16,9,256,128]{2,3,1,0:T(8,128)(2,1)} async-done(((bf16[16,9,256,128]{2,3,1,0:T(8,128)(2,1)}), bf16[16,9,256,128]{2,3,1,0:T(8,128)(2,1)}, u32[]{:S(2)}, u32[]{:S(2)}) %all-to-all-start.1) | async-done | bytes 9437216 | tf_op jit(solution)/shard_map/all_to_all | solution.py:61
  267.1 10.2 %fusion.20 = f32[16,9,256,64]{2,3,1,0:T(8,128)} fusion(bf16[256,64]{0,1:T(8,128)(2,1)S(1)} %copy-done.1, bf16[16,9,256,128]{2,3,1,0:T(8,128)(2,1)} %all-to-all-done.1), kind=kOutput, calls=%fused_computation.25 | convolution fusion | flops 604569600 | bytes 18907136 | tf_op jit(solution)/shard_map/...br,...rk->...bk/dot_general | solution.py:18
  277.4 11.7 %bitcast_add_fusion.5 = (f32[4,256,64]{1,0,2:T(4,128)S(1)}, f32[4,256,64]{1,0,2:T(4,128)S(1)}) fusion(f32[4,64,256]{2,1,0:T(8,128)S(1)} %fusion.52, f32[144,256,64]{1,2,0:T(8,128)} %bitcast.112, s32[144]{0:T(256)S(1)} %eq.34), kind=kOutput, calls=%fused_computation.48 | convolution fusion | flops 113312320 | bytes 10224192 | tf_op jit(solution)/shard_map/sp,pbk->sbk/dot_general | solution.py:79
  289.5 23.5 %custom-call.8 = f32[4,64,64]{2,1,0:T(8,128)S(1)} custom-call(f32[4,64,64]{2,1,0:T(8,128)S(1)} %fusion.65), custom_call_target="Cholesky" | custom-call | tf_op jit(solution)/shard_map/jit(cholesky)/cholesky | solution.py:25
  313.2 20.1 %custom-call.9 = f32[4,1,64,64]{2,3,1,0:T(8,128)S(1)} custom-call(f32[4,1,64,64]{3,2,1,0:T(8,128)S(1)} %select_bitcast_fusion.1), custom_call_target="InvertDiagBlocksLowerTriangular" | custom-call | tf_op jit(solution)/shard_map/jit(_solve_triangular)/vmap()/triangular_solve | solution.py:26
  334.0 3.7 convolution_convert_fusion.2
  337.7 9.4 %fusion.89 = (bf16[16,9,256,64]{2,3,1,0:T(8,128)(2,1)}, bf16[16,9,256,64]{2,3,1,0:T(8,128)(2,1)}) fusion(bf16[16,9,256,128]{2,3,1,0:T(8,128)(2,1)} %all-to-all-done.1), kind=kLoop, calls=%fused_computation.86 | loop fusion | bytes 18874368 | tf_op jit(solution)/shard_map/slice | solution.py:66
  347.1 12.5 %fusion.18 = f32[144,256,64]{1,2,0:T(8,128)} fusion(bf16[144,256,64]{1,2,0:T(8,128)(2,1)} %bitcast.108, bf16[144,256,64]{1,2,0:T(8,128)(2,1)} %bitcast.105, bf16[144,256,64]{1,0,2:T(8,128)(2,1)} %convolution_convert_fusion.2), kind=kOutput, calls=%fused_computation.23 | convolution fusion | flops 604569600 | bytes 23592960 | tf_op jit(solution)/shard_map/pbr,prk->pbk/dot_general | solution.py:31
  359.6 11.8 %fusion.45 = bf16[4,256,64]{1,0,2:T(4,128)(2,1)S(1)} fusion(f32[144,256,64]{1,2,0:T(8,128)} %fusion.18, f32[4,64,256]{2,1,0:T(8,128)S(1)} %fusion.53, s32[144]{0:T(256)S(1)} %eq.34), kind=kOutput, calls=%fused_computation.34 | convolution fusion | flops 113377856 | bytes 9830976 | tf_op jit(solution)/shard_map/sp,pbk->sbk/dot_general | solution.py:79
  371.4 3.7 convolution_convert_fusion.1
  375.4 12.5 %fusion.16 = f32[144,256,64]{1,2,0:T(8,128)} fusion(bf16[144,256,64]{1,2,0:T(8,128)(2,1)} %bitcast.106, bf16[144,256,64]{1,2,0:T(8,128)(2,1)} %bitcast.109, bf16[144,256,64]{1,0,2:T(8,128)(2,1)} %convolution_convert_fusion.1), kind=kOutput, calls=%fused_computation.21 | convolution fusion | flops 604569600 | bytes 23592960 | tf_op jit(solution)/shard_map/pbr,prk->pbk/dot_general | solution.py:31
  387.9 11.7 %bitcast_add_fusion.2 = (f32[4,256,64]{1,0,2:T(4,128)S(1)}, f32[4,256,64]{1,0,2:T(4,128)S(1)}) fusion(f32[4,64,256]{2,1,0:T(8,128)S(1)} %fusion.54, f32[144,256,64]{1,2,0:T(8,128)} %fusion.16, s32[144]{0:T(256)S(1)} %eq.34), kind=kOutput, calls=%fused_computation.46 | convolution fusion | flops 113312320 | bytes 10224192 | tf_op jit(solution)/shard_map/sp,pbk->sbk/dot_general | solution.py:79
  400.1 23.5 %custom-call.10 = f32[4,64,64]{2,1,0:T(8,128)S(1)} custom-call(f32[4,64,64]{2,1,0:T(8,128)S(1)} %fusion.63), custom_call_target="Cholesky" | custom-call | tf_op jit(solution)/shard_map/jit(cholesky)/cholesky | solution.py:25
  423.8 19.9 %custom-call.11 = f32[4,1,64,64]{2,3,1,0:T(8,128)S(1)} custom-call(f32[4,1,64,64]{3,2,1,0:T(8,128)S(1)} %select_bitcast_fusion), custom_call_target="InvertDiagBlocksLowerTriangular" | custom-call | tf_op jit(solution)/shard_map/jit(_solve_triangular)/vmap()/triangular_solve | solution.py:26
  444.4 3.7 convolution_convert_fusion
  448.0 12.5 %fusion.14 = f32[144,256,64]{1,2,0:T(8,128)} fusion(bf16[144,256,64]{1,2,0:T(8,128)(2,1)} %bitcast.110, bf16[144,256,64]{1,2,0:T(8,128)(2,1)} %bitcast.107, bf16[144,256,64]{1,0,2:T(8,128)(2,1)} %convolution_convert_fusion), kind=kOutput, calls=%fused_computation.19 | convolution fusion | flops 604569600 | bytes 23592960 | tf_op jit(solution)/shard_map/pbr,prk->pbk/dot_general | solution.py:31
  460.5 11.7 %fusion.48 = bf16[256,4,64]{0,1,2:T(4,128)(2,1)S(1)} fusion(f32[144,256,64]{1,2,0:T(8,128)} %fusion.14, f32[4,64,256]{2,1,0:T(8,128)S(1)} %fusion.55, s32[144]{0:T(256)S(1)} %eq.34), kind=kOutput, calls=%fused_computation.35 | convolution fusion | flops 113377856 | bytes 9830976 | tf_op jit(solution)/shard_map/sp,pbk->sbk/dot_general | solution.py:79
  473.9 48.0 %all-gather.2.cloned.1.call-done = bf16[256,4096]{0,1:T(8,128)(2,1)} async-done(((bf16[256,256]{0,1:T(8,128)(2,1)}), bf16[256,4096]{0,1:T(8,128)(2,1)}) %all-gather.2.cloned.1.call-update) | async-done | bytes 2097168 | tf_op jit(solution)/shard_map/all_gather | solution.py:110
  521.9 4.3 fusion.90
  (45 shorter events, 11.0 us)
Async XLA Ops:
  7.2 465.1 %copy-start = (bf16[256,256]{1,0:T(8,128)(2,1)S(1)}, bf16[256,256]{1,0:T(8,128)(2,1)}, u32[]{:S(2)}) copy-start(bf16[256,256]{1,0:T(8,128)(2,1)} %param.16) | copy-start | bytes 393220
  11.2 41.8 %all-to-all-start = ((s32[16,1,9]{2,1,0:T(1,128)}), s32[16,1,9]{2,1,0:T(1,128)S(1)}, u32[]{:S(2)}, u32[]{:S(2)}) async-start(s32[16,1,9]{2,1,0:T(1,128)} %bitcast.3), calls=%async_computation | async-start | bytes 16384 | tf_op jit(solution)/shard_map/all_to_all | solution.py:62
  53.0 7.7 %copy-start.2 = (bf16[256,256]{1,0:T(8,128)(2,1)S(1)}, bf16[256,256]{1,0:T(8,128)(2,1)}, u32[]{:S(2)}) copy-start(bf16[256,256]{1,0:T(8,128)(2,1)} %param.14) | copy-start | bytes 393220
  53.0 7.8 %copy-start.3 = (bf16[256,256]{1,0:T(8,128)(2,1)S(1)}, bf16[256,256]{1,0:T(8,128)(2,1)}, u32[]{:S(2)}) copy-start(bf16[256,256]{1,0:T(8,128)(2,1)} %param.13) | copy-start | bytes 393220
  53.0 7.9 %copy-start.1 = (bf16[256,64]{0,1:T(8,128)(2,1)S(1)}, bf16[256,64]{0,1:T(8,128)(2,1)}, u32[]{:S(2)}) copy-start(bf16[256,64]{0,1:T(8,128)(2,1)} %param.15) | copy-start | bytes 98308
  53.1 214.1 %all-to-all-start.1 = ((bf16[16,9,256,128]{2,3,1,0:T(8,128)(2,1)}), bf16[16,9,256,128]{2,3,1,0:T(8,128)(2,1)}, u32[]{:S(2)}, u32[]{:S(2)}) async-start(bf16[16,9,256,128]{2,3,1,0:T(8,128)(2,1)} %bitcast.111), calls=%async_computation.1 | async-start | bytes 18874368 | tf_op jit(solution)/shard_map/all_to_all | solution.py:61
  60.5 461.5 %all-gather.2.cloned.1.call-start = ((), (), s32[]{:S(2)}) async-start(), calls=%async_computation.2 | async-start | bytes 2228224 | tf_op jit(solution)/shard_map/all_gather | solution.py:110
Sparse Core Ops, SparseCore 0:
  473.3 48.6 all-gather.1
where the time goes:
time: 537 us; the launch traced here: 533 us
  waiting for transfers between devices  253 us (47%)
  matrix products  114 us (21%)
  other arithmetic  90.4 us (17%)
  local copies, waits for them, and re-layouts  46.1 us (9%)
  starting transfers between devices  16.2 us (3%)
  between operations  14.5 us (3%)
    all_to_all x1, waiting for transfers between devices, shards(): lax.all_to_all(outgoing, 'front', split_axis=0, concat_axis=0, tiled=True)  204 us
    all_gather x1, waiting for transfers between devices, shards(): lax.all_gather(pivoted, 'tile', axis=1, tiled=True)  48 us
    another operation x7, other arithmetic, orthonormal_basis(): lower = jnp.linalg.cholesky(gram_matrix)  47.2 us
    dot_general x4, matrix products, collect(): jnp.einsum('sp,pbk->sbk', owner_float, per_piece, precision=lax.Precision...  46.8 us
    another operation x5, other arithmetic, orthonormal_basis(): jax.scipy.linalg.solve_triangular(lower, jnp.swapaxes(block_unit, 1, 2),...  40.1 us
    dot_general x6, matrix products, expand(): jnp.einsum('pbr,prk->pbk', factor, small, preferred_element_type=jnp.floa...  38.4 us
    scatter x2, local copies, waits for them, and re-layouts, shards(): outgoing = jnp.zeros((fronts * CAP, B, 2 * R), jnp.bfloat16).at[places].s...  27.3 us
    dot_general x3, matrix products, select(): jnp.einsum('eo,elj->olj', owner_halves, field_values, preferred_element_t...  11 us
  transfers between devices with their start and end apart: 3, of which 2 were waited for; matrix products, arithmetic and copies ran while one was open for 7% of the time, Pallas kernels for 0%

commit v1 on v0

--- a/solution.py
+++ b/solution.py
@@ -107,7 +107,9 @@
     cores = jnp.einsum(
         "bi,bj->ij",
         coeff,
-        lax.all_gather(pivoted, "tile", axis=1, tiled=True),
+        jnp.concatenate(
+            lax.all_to_all(jnp.stack([pivoted] * lax.axis_size("tile")), "tile", 0, 0), axis=1
+        ),
         preferred_element_type=jnp.float32,
     )
     return (coeff, cores)

time: 537 us -> 514 us (0.957)
  waiting for transfers between devices: 253 us -> 231 us
  between operations: 14.5 us -> 1.17 us
  starting transfers between devices: 16.2 us -> 23.6 us
    all_gather x1 -> x0, waiting for transfers between devices: 48 us -> none  [shards(): lax.all_gather(pivoted, 'tile', axis=1, tiled=True)]
    all_to_all x0 -> x1, waiting for transfers between devices: none -> 26.1 us  [shards(): lax.all_to_all(jnp.stack([pivoted] * lax.axis_size('tile')), 'tile', 0, 0)]
    all_to_all x0 -> x1, starting transfers between devices: none -> 7.38 us  [shards(): lax.all_to_all(jnp.stack([pivoted] * lax.axis_size('tile')), 'tile', 0, 0)]
where the time goes in v1:
time: 514 us; the launch traced here: 505 us
  waiting for transfers between devices  231 us (45%)
  matrix products  112 us (22%)
  other arithmetic  90.2 us (18%)
  local copies, waits for them, and re-layouts  47.5 us (9%)
  starting transfers between devices  23.6 us (5%)
    all_to_all x1, waiting for transfers between devices, shards(): lax.all_to_all(outgoing, 'front', split_axis=0, concat_axis=0, tiled=True)  205 us
    dot_general x4, matrix products, collect(): jnp.einsum('sp,pbk->sbk', owner_float, per_piece, precision=lax.Precision...  47.3 us
    another operation x7, other arithmetic, orthonormal_basis(): lower = jnp.linalg.cholesky(gram_matrix)  47.2 us
    another operation x5, other arithmetic, orthonormal_basis(): jax.scipy.linalg.solve_triangular(lower, jnp.swapaxes(block_unit, 1, 2),...  39.9 us
    dot_general x6, matrix products, expand(): jnp.einsum('pbr,prk->pbk', factor, small, preferred_element_type=jnp.floa...  38.4 us
    scatter x2, local copies, waits for them, and re-layouts, shards(): outgoing = jnp.zeros((fronts * CAP, B, 2 * R), jnp.bfloat16).at[places].s...  27.2 us
    all_to_all x1, waiting for transfers between devices, shards(): lax.all_to_all(jnp.stack([pivoted] * lax.axis_size('tile')), 'tile', 0, 0)  26.1 us
    dot_general x3, matrix products, select(): jnp.einsum('eo,elj->olj', owner_halves, field_values, preferred_element_t...  11 us
  transfers between devices with their start and end apart: 3, of which 2 were waited for; matrix products, arithmetic and copies ran while one was open for 7% of the time, Pallas kernels for 0%

profile of v1, /device:TPU:2, one launch (start us, length us, event | category | flops | bytes accessed | tf_op | source)
XLA Modules:
  0.0 505.2 jit_solution(9617506911736732999)
XLA Ops:
  4.7 8.6 %all-to-all-start = ((s32[16,1,9]{2,1,0:T(1,128)}), s32[16,1,9]{2,1,0:T(1,128)S(1)}, u32[]{:S(2)}, u32[]{:S(2)}) async-start(s32[16,1,9]{2,1,0:T(1,128)} %bitcast.3), calls=%async_computation | async-start | bytes 16384 | tf_op jit(solution)/shard_map/all_to_all | solution.py:62
  13.2 6.0 %broadcast_in_dim.7 = bf16[144,256,128]{2,1,0:T(8,128)(2,1)} broadcast(bf16[]{:T(256)} %constant.46.clone.1), dimensions={} | broadcast | bytes 9437186 | tf_op jit(solution)/shard_map/broadcast_in_dim | solution.py:49
  19.2 14.5 %scatter_fusion = bf16[144,256,128]{2,1,0:T(8,128)(2,1)} fusion(bf16[144,256,128]{2,1,0:T(8,128)(2,1)} %broadcast_in_dim.7, s32[72]{0:T(128)S(1)} %fusion.76, bf16[72,256,128]{2,1,0:T(8,128)(2,1)} %param.10), kind=kCustom, calls=%fused_computation.1 | custom fusion | bytes 14156064 | tf_op jit(solution)/shard_map/scatter | solution.py:51
  33.7 12.7 %copy.126 = bf16[144,256,128]{1,2,0:T(8,128)(2,1)} copy(bf16[144,256,128]{2,1,0:T(8,128)(2,1)} %scatter_fusion) | data formatting | bytes 18874368 | tf_op jit(solution)/shard_map/scatter | solution.py:51
  46.5 7.7 %all-to-all-start.1 = ((bf16[16,9,256,128]{2,3,1,0:T(8,128)(2,1)}), bf16[16,9,256,128]{2,3,1,0:T(8,128)(2,1)}, u32[]{:S(2)}, u32[]{:S(2)}) async-start(bf16[16,9,256,128]{2,3,1,0:T(8,128)(2,1)} %bitcast.114), calls=%async_computation.1 | async-start | bytes 18874368 | tf_op jit(solution)/shard_map/all_to_all | solution.py:61
  56.1 204.7 %all-to-all-done.1 = bf16[16,9,256,128]{2,3,1,0:T(8,128)(2,1)} async-done(((bf16[16,9,256,128]{2,3,1,0:T(8,128)(2,1)}), bf16[16,9,256,128]{2,3,1,0:T(8,128)(2,1)}, u32[]{:S(2)}, u32[]{:S(2)}) %all-to-all-start.1) | async-done | bytes 9437216 | tf_op jit(solution)/shard_map/all_to_all | solution.py:61
  260.8 10.2 %fusion.20 = f32[16,9,256,64]{2,3,1,0:T(8,128)} fusion(bf16[256,64]{0,1:T(8,128)(2,1)S(1)} %copy-done.1, bf16[16,9,256,128]{2,3,1,0:T(8,128)(2,1)} %all-to-all-done.1), kind=kOutput, calls=%fused_computation.25 | convolution fusion | flops 604569600 | bytes 18907136 | tf_op jit(solution)/shard_map/...br,...rk->...bk/dot_general | solution.py:18
  271.0 11.7 %bitcast_add_fusion.5 = (f32[4,256,64]{1,0,2:T(4,128)S(1)}, f32[4,256,64]{1,0,2:T(4,128)S(1)}) fusion(f32[4,64,256]{2,1,0:T(8,128)S(1)} %fusion.52, f32[144,256,64]{1,2,0:T(8,128)} %bitcast.115, s32[144]{0:T(256)S(1)} %eq.34), kind=kOutput, calls=%fused_computation.48 | convolution fusion | flops 113312320 | bytes 10224192 | tf_op jit(solution)/shard_map/sp,pbk->sbk/dot_general | solution.py:79
  283.2 23.5 %custom-call.8 = f32[4,64,64]{2,1,0:T(8,128)S(1)} custom-call(f32[4,64,64]{2,1,0:T(8,128)S(1)} %fusion.65), custom_call_target="Cholesky" | custom-call | tf_op jit(solution)/shard_map/jit(cholesky)/cholesky | solution.py:25
  306.9 20.1 %custom-call.9 = f32[4,1,64,64]{2,3,1,0:T(8,128)S(1)} custom-call(f32[4,1,64,64]{3,2,1,0:T(8,128)S(1)} %select_bitcast_fusion.1), custom_call_target="InvertDiagBlocksLowerTriangular" | custom-call | tf_op jit(solution)/shard_map/jit(_solve_triangular)/vmap()/triangular_solve | solution.py:26
  327.7 3.7 convolution_convert_fusion.2
  331.3 9.4 %fusion.89 = (bf16[16,9,256,64]{2,3,1,0:T(8,128)(2,1)}, bf16[16,9,256,64]{2,3,1,0:T(8,128)(2,1)}) fusion(bf16[16,9,256,128]{2,3,1,0:T(8,128)(2,1)} %all-to-all-done.1), kind=kLoop, calls=%fused_computation.86 | loop fusion | bytes 18874368 | tf_op jit(solution)/shard_map/slice | solution.py:66
  340.7 12.5 %fusion.18 = f32[144,256,64]{1,2,0:T(8,128)} fusion(bf16[144,256,64]{1,2,0:T(8,128)(2,1)} %bitcast.111, bf16[144,256,64]{1,2,0:T(8,128)(2,1)} %bitcast.108, bf16[144,256,64]{1,0,2:T(8,128)(2,1)} %convolution_convert_fusion.2), kind=kOutput, calls=%fused_computation.23 | convolution fusion | flops 604569600 | bytes 23592960 | tf_op jit(solution)/shard_map/pbr,prk->pbk/dot_general | solution.py:31
  353.3 11.8 %fusion.45 = bf16[4,256,64]{1,0,2:T(4,128)(2,1)S(1)} fusion(f32[144,256,64]{1,2,0:T(8,128)} %fusion.18, f32[4,64,256]{2,1,0:T(8,128)S(1)} %fusion.53, s32[144]{0:T(256)S(1)} %eq.34), kind=kOutput, calls=%fused_computation.34 | convolution fusion | flops 113377856 | bytes 9830976 | tf_op jit(solution)/shard_map/sp,pbk->sbk/dot_general | solution.py:79
  365.1 3.7 convolution_convert_fusion.1
  369.0 12.5 %fusion.16 = f32[144,256,64]{1,2,0:T(8,128)} fusion(bf16[144,256,64]{1,2,0:T(8,128)(2,1)} %bitcast.109, bf16[144,256,64]{1,2,0:T(8,128)(2,1)} %bitcast.112, bf16[144,256,64]{1,0,2:T(8,128)(2,1)} %convolution_convert_fusion.1), kind=kOutput, calls=%fused_computation.21 | convolution fusion | flops 604569600 | bytes 23592960 | tf_op jit(solution)/shard_map/pbr,prk->pbk/dot_general | solution.py:31
  381.6 11.9 %bitcast_add_fusion.2 = (f32[4,256,64]{1,0,2:T(4,128)S(1)}, f32[4,256,64]{1,0,2:T(4,128)S(1)}) fusion(f32[4,64,256]{2,1,0:T(8,128)S(1)} %fusion.54, f32[144,256,64]{1,2,0:T(8,128)} %fusion.16, s32[144]{0:T(256)S(1)} %eq.34), kind=kOutput, calls=%fused_computation.46 | convolution fusion | flops 113312320 | bytes 10224192 | tf_op jit(solution)/shard_map/sp,pbk->sbk/dot_general | solution.py:79
  393.9 23.5 %custom-call.10 = f32[4,64,64]{2,1,0:T(8,128)S(1)} custom-call(f32[4,64,64]{2,1,0:T(8,128)S(1)} %fusion.63), custom_call_target="Cholesky" | custom-call | tf_op jit(solution)/shard_map/jit(cholesky)/cholesky | solution.py:25
  417.6 19.7 %custom-call.11 = f32[4,1,64,64]{2,3,1,0:T(8,128)S(1)} custom-call(f32[4,1,64,64]{3,2,1,0:T(8,128)S(1)} %select_bitcast_fusion), custom_call_target="InvertDiagBlocksLowerTriangular" | custom-call | tf_op jit(solution)/shard_map/jit(_solve_triangular)/vmap()/triangular_solve | solution.py:26
  438.1 3.7 convolution_convert_fusion
  441.7 12.5 %fusion.14 = f32[144,256,64]{1,2,0:T(8,128)} fusion(bf16[144,256,64]{1,2,0:T(8,128)(2,1)} %bitcast.113, bf16[144,256,64]{1,2,0:T(8,128)(2,1)} %bitcast.110, bf16[144,256,64]{1,0,2:T(8,128)(2,1)} %convolution_convert_fusion), kind=kOutput, calls=%fused_computation.19 | convolution fusion | flops 604569600 | bytes 23592960 | tf_op jit(solution)/shard_map/pbr,prk->pbk/dot_general | solution.py:31
  454.2 11.9 %fusion.48 = bf16[256,4,64]{0,1,2:T(4,128)(2,1)S(1)} fusion(f32[144,256,64]{1,2,0:T(8,128)} %fusion.14, f32[4,64,256]{2,1,0:T(8,128)S(1)} %fusion.55, s32[144]{0:T(256)S(1)} %eq.34), kind=kOutput, calls=%fused_computation.35 | convolution fusion | flops 113377856 | bytes 9830976 | tf_op jit(solution)/shard_map/sp,pbk->sbk/dot_general | solution.py:79
  467.9 7.4 %all-to-all-start.2 = ((bf16[16,256,256]{1,2,0:T(8,128)(2,1)}), bf16[16,256,256]{1,2,0:T(8,128)(2,1)S(1)}, u32[]{:S(2)}, u32[]{:S(2)}) async-start(bf16[16,256,256]{1,2,0:T(8,128)(2,1)} %stack.2), calls=%async_computation.2 | async-start | bytes 4194304 | tf_op jit(solution)/shard_map/all_to_all | solution.py:111
  476.1 26.1 %all-to-all-done.2 = bf16[16,256,256]{1,2,0:T(8,128)(2,1)S(1)} async-done(((bf16[16,256,256]{1,2,0:T(8,128)(2,1)}), bf16[16,256,256]{1,2,0:T(8,128)(2,1)S(1)}, u32[]{:S(2)}, u32[]{:S(2)}) %all-to-all-start.2) | async-done | bytes 2097184 | tf_op jit(solution)/shard_map/all_to_all | solution.py:111
  (45 shorter events, 14.4 us)
Async XLA Ops:
  0.6 465.5 %copy-start = (bf16[256,256]{1,0:T(8,128)(2,1)S(1)}, bf16[256,256]{1,0:T(8,128)(2,1)}, u32[]{:S(2)}) copy-start(bf16[256,256]{1,0:T(8,128)(2,1)} %param.16) | copy-start | bytes 393220
  4.7 41.8 %all-to-all-start = ((s32[16,1,9]{2,1,0:T(1,128)}), s32[16,1,9]{2,1,0:T(1,128)S(1)}, u32[]{:S(2)}, u32[]{:S(2)}) async-start(s32[16,1,9]{2,1,0:T(1,128)} %bitcast.3), calls=%async_computation | async-start | bytes 16384 | tf_op jit(solution)/shard_map/all_to_all | solution.py:62
  46.5 7.7 %copy-start.2 = (bf16[256,256]{1,0:T(8,128)(2,1)S(1)}, bf16[256,256]{1,0:T(8,128)(2,1)}, u32[]{:S(2)}) copy-start(bf16[256,256]{1,0:T(8,128)(2,1)} %param.14) | copy-start | bytes 393220
  46.5 7.8 %copy-start.3 = (bf16[256,256]{1,0:T(8,128)(2,1)S(1)}, bf16[256,256]{1,0:T(8,128)(2,1)}, u32[]{:S(2)}) copy-start(bf16[256,256]{1,0:T(8,128)(2,1)} %param.13) | copy-start | bytes 393220
  46.5 8.0 %copy-start.1 = (bf16[256,64]{0,1:T(8,128)(2,1)S(1)}, bf16[256,64]{0,1:T(8,128)(2,1)}, u32[]{:S(2)}) copy-start(bf16[256,64]{0,1:T(8,128)(2,1)} %param.15) | copy-start | bytes 98308
  46.5 214.3 %all-to-all-start.1 = ((bf16[16,9,256,128]{2,3,1,0:T(8,128)(2,1)}), bf16[16,9,256,128]{2,3,1,0:T(8,128)(2,1)}, u32[]{:S(2)}, u32[]{:S(2)}) async-start(bf16[16,9,256,128]{2,3,1,0:T(8,128)(2,1)} %bitcast.114), calls=%async_computation.1 | async-start | bytes 18874368 | tf_op jit(solution)/shard_map/all_to_all | solution.py:61
  467.9 34.2 %all-to-all-start.2 = ((bf16[16,256,256]{1,2,0:T(8,128)(2,1)}), bf16[16,256,256]{1,2,0:T(8,128)(2,1)S(1)}, u32[]{:S(2)}, u32[]{:S(2)}) async-start(bf16[16,256,256]{1,2,0:T(8,128)(2,1)} %stack.2), calls=%async_computation.2 | async-start | bytes 4194304 | tf_op jit(solution)/shard_map/all_to_all | solution.py:111
